TPU v7x, 256 devices: a whole 4x4x8 slice. The times are simulated.
256 devices in a mesh: dp: 4 (over x), expert: 64 (over z, y, core).
Axes of the slice: x: 4, y: 4, z: 8, core: 2. Of those that a mesh axis runs over, the one named last changes fastest.
Arguments:
- cell_table: bfloat16 [524288, 256], P(('dp', 'expert')), may hold values from -6 to 6
- sample_index: int32 [262144], P(('dp', 'expert')), may hold values from 0 to 2047
- region: int32 [262144, 1], P(('dp', 'expert')), may hold values from 0 to 63; in each aligned block of 1024 rows (0 to 1023, 1024 to 2047, ...) at most 32 rows name the same one
- targets: bfloat16 [262144, 256], P(('dp', 'expert')), may hold values from -6 to 6
- trunk_weight: bfloat16 [256, 256], replicated, may hold values from -0.375 to 0.375
- expert_params: float32 [64, 2, 256, 2048], P('expert', None, None, 'dp'), may hold values from -0.375 to 0.375
- first_moment: float32 [64, 2, 256, 2048], P('expert', None, None, 'dp'), may hold values from -4 to 4
- second_moment: float32 [64, 2, 256, 2048], P('expert', None, None, 'dp'), may hold values from 0.05 to 1
Outputs:
- trunk_grad: float32 [256, 256], replicated
- row_loss: float32 [262144], P(('dp', 'expert'))
- new_params: float32 [64, 2, 256, 2048], P('expert', None, None, 'dp')
- new_first: float32 [64, 2, 256, 2048], P('expert', None, None, 'dp')
- new_second: float32 [64, 2, 256, 2048], P('expert', None, None, 'dp')
Inputs may be any that keep to these rules, and one draw needn't show every extreme that they name: In the 1024 rows of one device no region is named more than 32 times; some region exactly 32 times. `sample_index`: indexes the rows of the same device's block of cell_table.
All inputs are finite; a program needn't handle non-finite values.
Results may differ from a plain program's by a relative error of at most 0.0044.
Values may be sent and summed in bfloat16 or wider, within the bound.
A program may use at most 128 MiB of HBM per device.

v0:
```python
import jax
import jax.numpy as jnp
from jax import lax
from jax.sharding import PartitionSpec as P

loss_scale = 1.0 / 32.0
beta_one = 0.9
beta_two = 0.999
learn_rate = 0.05
adam_eps = 1e-08
adam_step = 10


def silu_slope(values):
    sigma = jax.nn.sigmoid(values)
    return sigma * (1.0 + values * (1.0 - sigma))


def adam_update(params, first, second, grads):
    first_new = beta_one * first + (1.0 - beta_one) * grads
    second_new = beta_two * second + (1.0 - beta_two) * grads * grads
    first_hat = first_new / (1.0 - beta_one**adam_step)
    second_hat = second_new / (1.0 - beta_two**adam_step)
    return (
        params - learn_rate * first_hat / (jnp.sqrt(second_hat) + adam_eps),
        first_new,
        second_new,
    )


def on_device(
    cell_table,
    sample_index,
    region,
    targets,
    trunk_weight,
    expert_params,
    first_moment,
    second_moment,
):
    rows = sample_index.shape[0]
    width = cell_table.shape[1]
    experts = lax.axis_size("expert")
    capacity = 2 * rows // experts
    features = jnp.take(cell_table, sample_index, axis=0)
    routed = region[:, 0]
    onehot = (routed[:, None] == jnp.arange(experts, dtype=jnp.int32)[None, :]).astype(jnp.int32)
    slots = jnp.sum(jnp.cumsum(onehot, axis=0) * onehot, axis=1) - 1
    places = routed * capacity + slots
    gathered = lax.all_gather(expert_params.astype(jnp.bfloat16), "dp", axis=3, tiled=True)
    w_up = gathered[0, 0]
    w_down = gathered[0, 1]
    payload = jnp.concatenate([features, targets], axis=1)
    packed = jnp.zeros((experts * capacity, 2 * width), jnp.bfloat16).at[places].set(payload)
    arrived = lax.all_to_all(
        packed.reshape(experts, capacity, 2 * width),
        "expert",
        split_axis=0,
        concat_axis=0,
        tiled=True,
    ).reshape(-1, 2 * width)
    feats = arrived[:, :width]
    there = arrived[:, width:]
    trunk_pre = jnp.dot(feats, trunk_weight, preferred_element_type=jnp.float32)
    trunk_out = (feats.astype(jnp.float32) + jax.nn.silu(trunk_pre)).astype(jnp.bfloat16)
    up_pre = jnp.dot(trunk_out, w_up, preferred_element_type=jnp.float32)
    hidden = jax.nn.silu(up_pre).astype(jnp.bfloat16)
    predicted = lax.dot_general(
        hidden, w_down, (((1,), (1,)), ((), ())), preferred_element_type=jnp.float32
    )
    errors = predicted - there.astype(jnp.float32)
    losses = jnp.sum(errors * errors, axis=1) * (0.5 * loss_scale)
    scaled = (errors * loss_scale).astype(jnp.bfloat16)
    back = lax.all_to_all(
        losses.reshape(experts, capacity), "expert", split_axis=0, concat_axis=0, tiled=True
    )
    row_loss = back.reshape(-1)[places]
    grad_down = lax.dot_general(
        scaled, hidden, (((0,), (0,)), ((), ())), preferred_element_type=jnp.float32
    )
    hidden_grad = jnp.dot(scaled, w_down, preferred_element_type=jnp.float32)
    pre_grad = (hidden_grad * silu_slope(up_pre)).astype(jnp.bfloat16)
    grad_up = lax.dot_general(
        trunk_out, pre_grad, (((0,), (0,)), ((), ())), preferred_element_type=jnp.float32
    )
    row_grad = lax.dot_general(
        pre_grad, w_up, (((1,), (1,)), ((), ())), preferred_element_type=jnp.float32
    ).astype(jnp.bfloat16)
    trunk_slope = (row_grad.astype(jnp.float32) * silu_slope(trunk_pre)).astype(jnp.bfloat16)
    trunk_local = lax.dot_general(
        feats, trunk_slope, (((0,), (0,)), ((), ())), preferred_element_type=jnp.float32
    )
    trunk_grad = lax.psum(trunk_local, ("dp", "expert"))
    grads = jnp.stack([grad_up, grad_down])[None]
    grad_shard = lax.psum_scatter(grads, "dp", scatter_dimension=3, tiled=True)
    new_params, new_first, new_second = adam_update(
        expert_params, first_moment, second_moment, grad_shard
    )
    return (trunk_grad, row_loss, new_params, new_first, new_second)


def solution(mesh):
    placed = (
        P(("dp", "expert"), None),
        P(("dp", "expert")),
        P(("dp", "expert"), None),
        P(("dp", "expert"), None),
        P(),
        P("expert", None, None, "dp"),
        P("expert", None, None, "dp"),
        P("expert", None, None, "dp"),
    )
    return jax.shard_map(
        on_device,
        mesh=mesh,
        in_specs=placed,
        out_specs=(
            P(),
            P(("dp", "expert")),
            P("expert", None, None, "dp"),
            P("expert", None, None, "dp"),
            P("expert", None, None, "dp"),
        ),
        check_vma=False,
    )
```

profile of v0, /device:TPU:2, one launch (start us, length us, event | category | flops | bytes accessed | tf_op | source)
XLA Modules:
  0.0 451.5 jit_solution(14048339895175946293)
XLA Ops:
  7.2 0.8 fusion.17
  8.0 0.7 compare_and_fusion
  8.7 0.7 fusion.16
  9.4 18.0 %reduce-window.6 = s32[64,8,128]{2,1,0:T(8,128)S(1)} reduce-window(s32[64,8,128]{2,1,0:T(8,128)S(1)} %fusion.16, s32[]{:T(128)} %constant.20.clone.1), window={size=1x1x128 pad=0_0x0_0x127_0}, to_apply=%region_0.1 | reduce-window | flops 8323072 | bytes 524292 | tf_op jit(solution)/shard_map/reduce-window
  28.1 3.9 gather_fusion
  32.2 6.7 %scatter_custom_fusion = bf16[2048,512]{1,0:T(8,128)(2,1)} fusion(s32[1024]{0:T(1024)S(1)} %bitcast.54, bf16[1024,256]{1,0:T(8,128)(2,1)S(1)} %copy-done.4, bf16[]{:T(256)} %constant.67, bf16[1024,256]{1,0:T(8,128)(2,1)S(1)} %broadcast_select_fusion, bf16[]{:T(256)} %constant.18.clone.1), kind=kCustom, calls=%fused_computation.22 | custom fusion | flops 2097152 | bytes 3145732 | tf_op jit(solution)/shard_map/scatter | solution.py:54
  38.9 12.1 %all-to-all-start = ((bf16[64,32,512]{2,1,0:T(8,128)(2,1)}), bf16[64,32,512]{2,1,0:T(8,128)(2,1)S(1)}, u32[]{:S(2)}, u32[]{:S(2)}) async-start(bf16[64,32,512]{2,1,0:T(8,128)(2,1)} %bitcast.6), calls=%async_computation | async-start | bytes 4194304 | tf_op jit(solution)/shard_map/all_to_all | solution.py:55
  51.1 2.1 convert_element_type.38
  53.5 48.9 %all-to-all-done = bf16[64,32,512]{2,1,0:T(8,128)(2,1)S(1)} async-done(((bf16[64,32,512]{2,1,0:T(8,128)(2,1)}), bf16[64,32,512]{2,1,0:T(8,128)(2,1)S(1)}, u32[]{:S(2)}, u32[]{:S(2)}) %all-to-all-start) | async-done | bytes 2097184 | tf_op jit(solution)/shard_map/all_to_all | solution.py:55
  102.4 1.7 fusion.12
  104.2 10.1 %multiply_convert_fusion.1 = (bf16[2048,2048]{1,0:T(8,128)(2,1)S(1)}, f32[2048,2048]{1,0:T(8,128)}) fusion(bf16[1,2,256,2048]{3,2,1,0:T(8,128)(2,1)} %all-gather.2.cloned.1.call-done, f32[2048,256]{1,0:T(8,128)} %fusion.12, bf16[2048,512]{1,0:T(8,128)(2,1)S(1)} %bitcast.46), kind=kOutput, calls=%fused_computation.4 | convolution fusion | flops 2172125184 | bytes 29360128 | tf_op jit(solution)/shard_map/dot_general | solution.py:66
  114.3 2.6 multiply_reduce_fusion
  116.9 2.3 convolution_bitcast_fusion
  119.3 13.3 %multiply_convert_fusion = bf16[2048,2048]{1,0:T(8,128)(2,1)} fusion(f32[2048,2048]{1,0:T(8,128)} %get-tuple-element.9, bf16[1,2,256,2048]{3,2,1,0:T(8,128)(2,1)S(1)} %copy-done.7, f32[2048,256]{1,0:T(8,128)S(1)} %get-tuple-element.11), kind=kOutput, calls=%fused_computation.3 | convolution fusion | flops 2186280960 | bytes 28311552 | tf_op jit(solution)/shard_map/dot_general | solution.py:81
  132.6 5.8 %convolution_bitcast_fusion.1 = f32[1,256,2048]{2,1,0:T(8,128)S(1)} fusion(bf16[2048,2048]{1,0:T(8,128)(2,1)} %multiply_convert_fusion, f32[2048,256]{1,0:T(8,128)S(1)} %copy-done.2, bf16[2048,512]{1,0:T(8,128)(2,1)S(1)} %bitcast.48), kind=kOutput, calls=%fused_computation.8 | convolution fusion | flops 2151153664 | bytes 13631488 | tf_op jit(solution)/shard_map/dot_general | solution.py:83
  138.4 2.2 maximum_bitcast_fusion
  141.3 5.6 %all-to-all-start.1 = ((f32[64,1,32]{2,1,0:T(1,128)}), f32[64,1,32]{2,1,0:T(1,128)S(1)}, u32[]{:S(2)}, u32[]{:S(2)}) async-start(f32[64,1,32]{2,1,0:T(1,128)} %bitcast.10), calls=%async_computation.1 | async-start | bytes 65536 | tf_op jit(solution)/shard_map/all_to_all | solution.py:74
  147.0 9.0 %fusion.9 = f32[256,256]{1,0:T(8,128)} fusion(bf16[2048,2048]{1,0:T(8,128)(2,1)} %multiply_convert_fusion, f32[2048,256]{1,0:T(8,128)} %fusion.12, bf16[1,2,256,2048]{3,2,1,0:T(8,128)(2,1)} %all-gather.2.cloned.1.call-done, bf16[2048,512]{1,0:T(8,128)(2,1)S(1)} %bitcast.49), kind=kOutput, calls=%fused_computation.29 | convolution fusion | flops 2421686272 | bytes 12845056 | tf_op jit(solution)/shard_map/dot_general | solution.py:90
  157.0 0.7 reduce.3
  157.8 10.5 %gather_fusion.1 = f32[1024]{0:T(1024)} fusion(f32[2048]{0:T(1024)S(1)} %reshape.69, s32[1024]{0:T(1024)S(1)} %broadcast_clamp_fusion), kind=kCustom, calls=%fused_computation.1 | custom fusion | bytes 12288 | tf_op jit(solution)/shard_map/gather | solution.py:77
  168.3 16.8 %reduce-scatter.2.cloned.1.call-done = f32[1,2,256,512]{3,2,1,0:T(8,128)} async-done(((f32[1,2,256,2048]{3,2,1,0:T(8,128)}), f32[1,2,256,512]{3,2,1,0:T(8,128)}) %reduce-scatter.2.cloned.1.call-update) | async-done | bytes 1048592 | tf_op jit(solution)/shard_map/reduce_scatter | solution.py:95
  185.1 3.7 divide_subtract_fusion
  188.8 254.6 %all-reduce.2.cloned.1.call-done = f32[256,256]{1,0:T(8,128)} async-done(((f32[256,256]{1,0:T(8,128)}), f32[256,256]{1,0:T(8,128)}) %all-reduce.2.cloned.1.call-update) | async-done | bytes 262160 | tf_op jit(solution)/shard_map/psum | solution.py:93
  443.3 1.7 copy.25
  (39 shorter events, 3.0 us)
Async XLA Ops:
  7.2 20.9 %copy-start = (bf16[2048,256]{1,0:T(8,128)(2,1)S(1)}, bf16[2048,256]{1,0:T(8,128)(2,1)}, u32[]{:S(2)}) copy-start(bf16[2048,256]{1,0:T(8,128)(2,1)} %param.8) | copy-start | bytes 3145732
  7.2 20.8 %copy-start.6 = (s32[1024,1]{0,1:T(1,128)S(1)}, s32[1024,1]{0,1:T(1,128)}, u32[]{:S(2)}) copy-start(s32[1024,1]{0,1:T(1,128)} %param.10) | copy-start | bytes 12292
  28.1 4.2 copy-start.4
  38.9 63.5 %all-to-all-start = ((bf16[64,32,512]{2,1,0:T(8,128)(2,1)}), bf16[64,32,512]{2,1,0:T(8,128)(2,1)S(1)}, u32[]{:S(2)}, u32[]{:S(2)}) async-start(bf16[64,32,512]{2,1,0:T(8,128)(2,1)} %bitcast.6), calls=%async_computation | async-start | bytes 4194304 | tf_op jit(solution)/shard_map/all_to_all | solution.py:55
  51.0 51.4 %copy-start.5 = (bf16[256,256]{1,0:T(8,128)(2,1)S(1)}, bf16[256,256]{1,0:T(8,128)(2,1)}, u32[]{:S(2)}) copy-start(bf16[256,256]{1,0:T(8,128)(2,1)} %param.12) | copy-start | bytes 393220
  51.1 53.1 %all-gather.2.cloned.1.call-start = ((), (), s32[]{:S(2)}) async-start(), calls=%async_computation.3 | async-start | bytes 2621440 | tf_op jit(solution)/shard_map/all_gather | solution.py:50
  53.2 131.8 %reduce-scatter.2.cloned.1.call-start = ((), (), s32[]{:S(2)}) async-start(), calls=%async_computation.5 | async-start | bytes 5242880 | tf_op jit(solution)/shard_map/reduce_scatter | solution.py:95
  104.1 10.1 %copy-start.7 = (bf16[1,2,256,2048]{3,2,1,0:T(8,128)(2,1)S(1)}, bf16[1,2,256,2048]{3,2,1,0:T(8,128)(2,1)}, u32[]{:S(2)}) copy-start(bf16[1,2,256,2048]{3,2,1,0:T(8,128)(2,1)} %all-gather.2.cloned.1.call-done) | copy-start | bytes 6291460
  119.3 13.3 %copy-start.2 = (f32[2048,256]{1,0:T(8,128)S(1)}, f32[2048,256]{1,0:T(8,128)}, u32[]{:S(2)}) copy-start(f32[2048,256]{1,0:T(8,128)} %fusion.12) | copy-start | bytes 6291460
  141.3 15.1 %all-to-all-start.1 = ((f32[64,1,32]{2,1,0:T(1,128)}), f32[64,1,32]{2,1,0:T(1,128)S(1)}, u32[]{:S(2)}, u32[]{:S(2)}) async-start(f32[64,1,32]{2,1,0:T(1,128)} %bitcast.10), calls=%async_computation.1 | async-start | bytes 65536 | tf_op jit(solution)/shard_map/all_to_all | solution.py:74
  146.9 296.4 %all-reduce.2.cloned.1.call-start = ((), (), s32[]{:S(2)}) async-start(), calls=%async_computation.4 | async-start | bytes 524288 | tf_op jit(solution)/shard_map/psum | solution.py:93
  157.8 27.3 %copy-start.1 = (f32[1,2,256,512]{3,2,1,0:T(8,128)S(1)}, f32[1,2,256,512]{3,2,1,0:T(8,128)}, u32[]{:S(2)}) copy-start(f32[1,2,256,512]{3,2,1,0:T(8,128)} %param.13) | copy-start | bytes 3145732
  157.8 27.3 %copy-start.3 = (f32[1,2,256,512]{3,2,1,0:T(8,128)S(1)}, f32[1,2,256,512]{3,2,1,0:T(8,128)}, u32[]{:S(2)}) copy-start(f32[1,2,256,512]{3,2,1,0:T(8,128)} %param.14) | copy-start | bytes 3145732
Sparse Core Ops, SparseCore 0:
  54.3 33.5 all-gather.1
  140.7 44.3 reduce-scatter.1
  192.0 251.2 all-reduce.1
where the time goes:
time: 452 us
  waiting for transfers between devices  321 us (71%)
  matrix products  44.9 us (10%)
  other arithmetic  36.1 us (8%)
  starting transfers between devices  18 us (4%)
  local copies, waits for them, and re-layouts  17.8 us (4%)
  between operations  13.9 us (3%)
    psum x1, waiting for transfers between devices, on_device(): trunk_grad = lax.psum(trunk_local, ('dp', 'expert'))  255 us
    all_to_all x1, waiting for transfers between devices, on_device(): lax.all_to_all(packed.reshape(experts, capacity, 2 * width), 'expert', sp...  48.9 us
    another operation x3, other arithmetic  18.2 us
    reduce_scatter x1, waiting for transfers between devices, on_device(): grad_shard = lax.psum_scatter(grads, 'dp', scatter_dimension=3, tiled=True)  16.8 us
    dot_general x1, matrix products, on_device(): hidden_grad = jnp.dot(scaled, w_down, preferred_element_type=jnp.float32)  13.3 us
    all_to_all x1, starting transfers between devices, on_device(): lax.all_to_all(packed.reshape(experts, capacity, 2 * width), 'expert', sp...  12.1 us
    gather x1, local copies, waits for them, and re-layouts, on_device(): row_loss = back.reshape(-1)[places]  10.5 us
    dot_general x1, matrix products, on_device(): up_pre = jnp.dot(trunk_out, w_up, preferred_element_type=jnp.float32)  10.1 us
  transfers between devices with their start and end apart: 5, of which 4 were waited for; matrix products, arithmetic and copies ran while one was open for 6% of the time, Pallas kernels for 0%

commit v1 on v0

--- a/solution.py
+++ b/solution.py
@@ -90,7 +90,7 @@
     trunk_local = lax.dot_general(
         feats, trunk_slope, (((0,), (0,)), ((), ())), preferred_element_type=jnp.float32
     )
-    trunk_grad = lax.psum(trunk_local, ("dp", "expert"))
+    trunk_grad = lax.psum(lax.psum(trunk_local, "expert"), "dp")
     grads = jnp.stack([grad_up, grad_down])[None]
     grad_shard = lax.psum_scatter(grads, "dp", scatter_dimension=3, tiled=True)
     new_params, new_first, new_second = adam_update(

time: 452 us -> 427 us (0.945)
  waiting for transfers between devices: 321 us -> 292 us
    psum x1 -> x2, waiting for transfers between devices: 255 us -> 184 us  [on_device(): trunk_grad = lax.psum(lax.psum(trunk_local, 'expert'), 'dp')]
    reduce_scatter x1, waiting for transfers between devices: 16.8 us -> 49.5 us  [on_device(): grad_shard = lax.psum_scatter(grads, 'dp', scatter_dimension=3, tiled=True)]
    all_to_all x1, waiting for transfers between devices: 0.48 us -> 9.45 us  [on_device(): lax.all_to_all(losses.reshape(experts, capacity), 'expert', split_axis=0,...]
  transfers between devices with their start and end apart: 5 -> 6, of which waited for: 4 -> 5; matrix products, arithmetic and copies ran while one was open for 6% -> 6% of each run, Pallas kernels for 0% -> 0%
where the time goes in v1:
time: 427 us; the launch traced here: 426 us
  waiting for transfers between devices  292 us (68%)
  matrix products  46 us (11%)
  other arithmetic  37.8 us (9%)
  local copies, waits for them, and re-layouts  17.8 us (4%)
  starting transfers between devices  17.8 us (4%)
  between operations  14 us (3%)
    psum x2, waiting for transfers between devices, on_device(): trunk_grad = lax.psum(lax.psum(trunk_local, 'expert'), 'dp')  184 us
    reduce_scatter x1, waiting for transfers between devices, on_device(): grad_shard = lax.psum_scatter(grads, 'dp', scatter_dimension=3, tiled=True)  49.5 us
    all_to_all x1, waiting for transfers between devices, on_device(): lax.all_to_all(packed.reshape(experts, capacity, 2 * width), 'expert', sp...  48.9 us
    another operation x3, other arithmetic  18.2 us
    dot_general x1, matrix products, on_device(): hidden_grad = jnp.dot(scaled, w_down, preferred_element_type=jnp.float32)  13.3 us
    all_to_all x1, starting transfers between devices, on_device(): lax.all_to_all(packed.reshape(experts, capacity, 2 * width), 'expert', sp...  12.1 us
    gather x1, local copies, waits for them, and re-layouts, on_device(): row_loss = back.reshape(-1)[places]  10.5 us
    dot_general x1, matrix products, on_device(): up_pre = jnp.dot(trunk_out, w_up, preferred_element_type=jnp.float32)  10.2 us
  transfers between devices with their start and end apart: 6, of which 5 were waited for; matrix products, arithmetic and copies ran while one was open for 6% of the time, Pallas kernels for 0%

profile of v1, /device:TPU:2, one launch (start us, length us, event | category | flops | bytes accessed | tf_op | source)
XLA Modules:
  0.0 425.5 jit_solution(17517683685203440981)
XLA Ops:
  7.2 0.8 fusion.17
  9.4 18.0 %reduce-window.6 = s32[64,8,128]{2,1,0:T(8,128)S(1)} reduce-window(s32[64,8,128]{2,1,0:T(8,128)S(1)} %fusion.16, s32[]{:T(128)} %constant.20.clone.1), window={size=1x1x128 pad=0_0x0_0x127_0}, to_apply=%region_0.1 | reduce-window | flops 8323072 | bytes 524292 | tf_op jit(solution)/shard_map/reduce-window
  28.1 3.9 gather_fusion
  32.2 6.7 %scatter_custom_fusion = bf16[2048,512]{1,0:T(8,128)(2,1)} fusion(s32[1024]{0:T(1024)S(1)} %bitcast.54, bf16[1024,256]{1,0:T(8,128)(2,1)S(1)} %copy-done.6, bf16[]{:T(256)} %constant.67, bf16[1024,256]{1,0:T(8,128)(2,1)S(1)} %broadcast_select_fusion, bf16[]{:T(256)} %constant.18.clone.1), kind=kCustom, calls=%fused_computation.22 | custom fusion | flops 2097152 | bytes 3145732 | tf_op jit(solution)/shard_map/scatter | solution.py:54
  38.9 12.1 %all-to-all-start = ((bf16[64,32,512]{2,1,0:T(8,128)(2,1)}), bf16[64,32,512]{2,1,0:T(8,128)(2,1)S(1)}, u32[]{:S(2)}, u32[]{:S(2)}) async-start(bf16[64,32,512]{2,1,0:T(8,128)(2,1)} %bitcast.6), calls=%async_computation | async-start | bytes 4194304 | tf_op jit(solution)/shard_map/all_to_all | solution.py:55
  51.1 2.1 convert_element_type.38
  53.5 48.9 %all-to-all-done = bf16[64,32,512]{2,1,0:T(8,128)(2,1)S(1)} async-done(((bf16[64,32,512]{2,1,0:T(8,128)(2,1)}), bf16[64,32,512]{2,1,0:T(8,128)(2,1)S(1)}, u32[]{:S(2)}, u32[]{:S(2)}) %all-to-all-start) | async-done | bytes 2097184 | tf_op jit(solution)/shard_map/all_to_all | solution.py:55
  102.4 2.0 fusion.12
  104.4 10.2 %multiply_convert_fusion.1 = (bf16[2048,2048]{1,0:T(8,128)(2,1)S(1)}, f32[2048,2048]{1,0:T(8,128)}) fusion(bf16[1,2,256,2048]{3,2,1,0:T(8,128)(2,1)} %all-gather.2.cloned.1.call-done, f32[2048,256]{1,0:T(8,128)} %fusion.12, bf16[2048,512]{1,0:T(8,128)(2,1)S(1)} %bitcast.46), kind=kOutput, calls=%fused_computation.4 | convolution fusion | flops 2172125184 | bytes 29360128 | tf_op jit(solution)/shard_map/dot_general | solution.py:66
  114.6 2.6 multiply_reduce_fusion
  117.2 2.3 convolution_bitcast_fusion
  119.6 13.3 %multiply_convert_fusion = bf16[2048,2048]{1,0:T(8,128)(2,1)} fusion(f32[2048,2048]{1,0:T(8,128)} %get-tuple-element.9, bf16[1,2,256,2048]{3,2,1,0:T(8,128)(2,1)S(1)} %copy-done.9, f32[2048,256]{1,0:T(8,128)S(1)} %get-tuple-element.11), kind=kOutput, calls=%fused_computation.3 | convolution fusion | flops 2186280960 | bytes 28311552 | tf_op jit(solution)/shard_map/dot_general | solution.py:81
  132.9 7.1 %convolution_bitcast_fusion.1 = f32[1,256,2048]{2,1,0:T(8,128)} fusion(bf16[2048,2048]{1,0:T(8,128)(2,1)} %multiply_convert_fusion, f32[2048,256]{1,0:T(8,128)S(1)} %copy-done.4, bf16[2048,512]{1,0:T(8,128)(2,1)S(1)} %bitcast.49), kind=kOutput, calls=%fused_computation.8 | convolution fusion | flops 2151153664 | bytes 13631488 | tf_op jit(solution)/shard_map/dot_general | solution.py:83
  140.0 8.5 %fusion.9 = f32[256,256]{1,0:T(8,128)} fusion(bf16[2048,2048]{1,0:T(8,128)(2,1)} %multiply_convert_fusion, f32[2048,256]{1,0:T(8,128)} %fusion.12, bf16[1,2,256,2048]{3,2,1,0:T(8,128)(2,1)} %all-gather.2.cloned.1.call-done, bf16[2048,512]{1,0:T(8,128)(2,1)} %bitcast.48), kind=kOutput, calls=%fused_computation.29 | convolution fusion | flops 2421686272 | bytes 12845056 | tf_op jit(solution)/shard_map/dot_general | solution.py:90
  148.6 3.9 maximum_bitcast_fusion
  153.2 5.3 %all-to-all-start.1 = ((f32[64,1,32]{2,1,0:T(1,128)}), f32[64,1,32]{2,1,0:T(1,128)S(1)}, u32[]{:S(2)}, u32[]{:S(2)}) async-start(f32[64,1,32]{2,1,0:T(1,128)} %bitcast.10), calls=%async_computation.1 | async-start | bytes 65536 | tf_op jit(solution)/shard_map/all_to_all | solution.py:74
  158.6 9.5 %all-to-all-done.1 = f32[64,1,32]{2,1,0:T(1,128)S(1)} async-done(((f32[64,1,32]{2,1,0:T(1,128)}), f32[64,1,32]{2,1,0:T(1,128)S(1)}, u32[]{:S(2)}, u32[]{:S(2)}) %all-to-all-start.1) | async-done | bytes 8224 | tf_op jit(solution)/shard_map/all_to_all | solution.py:74
  168.6 0.7 reduce.3
  169.4 10.5 %gather_fusion.1 = f32[1024]{0:T(1024)} fusion(f32[2048]{0:T(1024)S(1)} %reshape.69, s32[1024]{0:T(1024)S(1)} %broadcast_clamp_fusion), kind=kCustom, calls=%fused_computation.1 | custom fusion | bytes 12288 | tf_op jit(solution)/shard_map/gather | solution.py:77
  179.9 139.0 %all-reduce.3.cloned.1.call-done = f32[256,256]{1,0:T(8,128)} async-done(((f32[256,256]{1,0:T(8,128)}), f32[256,256]{1,0:T(8,128)}) %all-reduce.3.cloned.1.call-update) | async-done | bytes 262160 | tf_op jit(solution)/shard_map/psum | solution.py:93
  319.0 49.5 %reduce-scatter.2.cloned.1.call-done = f32[1,2,256,512]{3,2,1,0:T(8,128)} async-done(((f32[1,2,256,2048]{3,2,1,0:T(8,128)}), f32[1,2,256,512]{3,2,1,0:T(8,128)}) %reduce-scatter.2.cloned.1.call-update) | async-done | bytes 1048592 | tf_op jit(solution)/shard_map/reduce_scatter | solution.py:95
  368.5 3.7 divide_subtract_fusion
  372.2 45.2 %all-reduce.5.cloned.1.call-done = f32[256,256]{1,0:T(8,128)} async-done(((f32[256,256]{1,0:T(8,128)}), f32[256,256]{1,0:T(8,128)}) %all-reduce.5.cloned.1.call-update) | async-done | bytes 262160 | tf_op jit(solution)/shard_map/psum | solution.py:93
  417.3 1.7 copy.26
  (46 shorter events, 3.9 us)
Async XLA Ops:
  7.2 20.9 %copy-start = (bf16[2048,256]{1,0:T(8,128)(2,1)S(1)}, bf16[2048,256]{1,0:T(8,128)(2,1)}, u32[]{:S(2)}) copy-start(bf16[2048,256]{1,0:T(8,128)(2,1)} %param.8) | copy-start | bytes 3145732
  7.2 20.8 %copy-start.8 = (s32[1024,1]{0,1:T(1,128)S(1)}, s32[1024,1]{0,1:T(1,128)}, u32[]{:S(2)}) copy-start(s32[1024,1]{0,1:T(1,128)} %param.10) | copy-start | bytes 12292
  28.1 4.2 copy-start.6
  38.9 63.5 %all-to-all-start = ((bf16[64,32,512]{2,1,0:T(8,128)(2,1)}), bf16[64,32,512]{2,1,0:T(8,128)(2,1)S(1)}, u32[]{:S(2)}, u32[]{:S(2)}) async-start(bf16[64,32,512]{2,1,0:T(8,128)(2,1)} %bitcast.6), calls=%async_computation | async-start | bytes 4194304 | tf_op jit(solution)/shard_map/all_to_all | solution.py:55
  51.0 51.4 %copy-start.7 = (bf16[256,256]{1,0:T(8,128)(2,1)S(1)}, bf16[256,256]{1,0:T(8,128)(2,1)}, u32[]{:S(2)}) copy-start(bf16[256,256]{1,0:T(8,128)(2,1)} %param.12) | copy-start | bytes 393220
  51.1 53.3 %all-gather.2.cloned.1.call-start = ((), (), s32[]{:S(2)}) async-start(), calls=%async_computation.3 | async-start | bytes 2621440 | tf_op jit(solution)/shard_map/all_gather | solution.py:50
  53.2 265.7 %all-reduce.3.cloned.1.call-start = ((), (), s32[]{:S(2)}) async-start(), calls=%async_computation.4 | async-start | bytes 524288 | tf_op jit(solution)/shard_map/psum | solution.py:93
  102.4 12.2 %copy-start.1 = (bf16[64,32,512]{2,1,0:T(8,128)(2,1)}, bf16[64,32,512]{2,1,0:T(8,128)(2,1)S(1)}, u32[]{:S(2)}) copy-start(bf16[64,32,512]{2,1,0:T(8,128)(2,1)S(1)} %all-to-all-done) | copy-start | bytes 6291460
  104.4 10.2 %copy-start.9 = (bf16[1,2,256,2048]{3,2,1,0:T(8,128)(2,1)S(1)}, bf16[1,2,256,2048]{3,2,1,0:T(8,128)(2,1)}, u32[]{:S(2)}) copy-start(bf16[1,2,256,2048]{3,2,1,0:T(8,128)(2,1)} %all-gather.2.cloned.1.call-done) | copy-start | bytes 6291460
  119.5 13.4 %copy-start.2 = (bf16[64,32,512]{2,1,0:T(8,128)(2,1)S(1)}, bf16[64,32,512]{2,1,0:T(8,128)(2,1)}, u32[]{:S(2)}) copy-start(bf16[64,32,512]{2,1,0:T(8,128)(2,1)} %copy-done.1) | copy-start | bytes 6291460
  119.5 13.3 %copy-start.4 = (f32[2048,256]{1,0:T(8,128)S(1)}, f32[2048,256]{1,0:T(8,128)}, u32[]{:S(2)}) copy-start(f32[2048,256]{1,0:T(8,128)} %fusion.12) | copy-start | bytes 6291460
  148.5 220.0 %reduce-scatter.2.cloned.1.call-start = ((), (), s32[]{:S(2)}) async-start(), calls=%async_computation.6 | async-start | bytes 5242880 | tf_op jit(solution)/shard_map/reduce_scatter | solution.py:95
  153.2 14.9 %all-to-all-start.1 = ((f32[64,1,32]{2,1,0:T(1,128)}), f32[64,1,32]{2,1,0:T(1,128)S(1)}, u32[]{:S(2)}, u32[]{:S(2)}) async-start(f32[64,1,32]{2,1,0:T(1,128)} %bitcast.10), calls=%async_computation.1 | async-start | bytes 65536 | tf_op jit(solution)/shard_map/all_to_all | solution.py:74
  158.5 258.8 %all-reduce.5.cloned.1.call-start = ((), (), s32[]{:S(2)}) async-start(), calls=%async_computation.5 | async-start | bytes 524288 | tf_op jit(solution)/shard_map/psum | solution.py:93
  169.4 199.1 %copy-start.3 = (f32[1,2,256,512]{3,2,1,0:T(8,128)S(1)}, f32[1,2,256,512]{3,2,1,0:T(8,128)}, u32[]{:S(2)}) copy-start(f32[1,2,256,512]{3,2,1,0:T(8,128)} %param.13) | copy-start | bytes 3145732
  169.4 199.1 %copy-start.5 = (f32[1,2,256,512]{3,2,1,0:T(8,128)S(1)}, f32[1,2,256,512]{3,2,1,0:T(8,128)}, u32[]{:S(2)}) copy-start(f32[1,2,256,512]{3,2,1,0:T(8,128)} %param.14) | copy-start | bytes 3145732
Sparse Core Ops, SparseCore 0:
  54.3 33.5 all-gather.1
  148.6 170.2 all-reduce.2
  321.7 46.7 reduce-scatter.1
  370.6 46.6 all-reduce.4
